TPU v7x, 256 devices: a whole 4x4x8 slice. The times are simulated.
256 devices in a mesh: grp: 8 (over y, x_hi), tok: 32 (over z, x_lo, core).
Axes of the slice: x: 4 (x_hi: 2, x_lo: 2; x = x_hi * 2 + x_lo), y: 4, z: 8, core: 2. Of those that a mesh axis runs over, the one named last changes fastest.
Arguments:
- layer_input: bfloat16 [8, 6144, 1536], P('grp', 'tok'), may hold values from -54 to 54
- attn_gain: float32 [1536], replicated, may hold values from 0.1 to 1.9
- w_query: bfloat16 [1536, 1536], P('tok'), may hold values from -0.15625 to 0.15625
- w_keyval: bfloat16 [1536, 1024], P('tok'), may hold values from -0.15625 to 0.15625
- w_output: bfloat16 [1536, 1536], P('tok'), may hold values from -0.15625 to 0.15625
- prefix_cache: bfloat16 [8, 512, 1024], P('grp', 'tok'), may hold values from -260 to 260
- lengths: int32 [8, 48], P('grp'), may hold values from 1 to 192, 6144 in all within a row
- moe_gain: float32 [1536], replicated, may hold values from 0.1 to 1.9
- w_router: bfloat16 [1536, 16], replicated, may hold values from -0.15625 to 0.15625
- routes: int32 [8, 6144, 2], P('grp', 'tok'), may hold values from 0 to 15, all different within a row; in each aligned block of 192 rows (0 to 191, 192 to 383, ..., all dimensions but the last counted through in order) at most 30 rows name the same one
- w_expert_in: bfloat16 [32, 1536, 1024], P('tok', 'grp'), may hold values from -0.15625 to 0.15625
- w_expert_out: bfloat16 [32, 512, 1536], P('tok', 'grp'), may hold values from -0.1875 to 0.1875
Outputs:
- hidden: bfloat16 [8, 6144, 1536], P('grp', 'tok')
- suffix_cache: bfloat16 [8, 6144, 1024], P('grp', 'tok')
Inputs may be any that keep to these rules, and one draw needn't show every extreme that they name: `lengths`: each row sums to 6144, and its largest length is 192. A token's 2 routes differ. Among the rows of one device no expert is named more than 30 times, a bound that some block reaches in some devices' rows.
All inputs are finite; a program needn't handle non-finite values.
Results may differ from a plain program's by a relative error of at most 0.0073.
The roundings to bfloat16 on the way count: a program that leaves them out, or rounds other values in their place, can miss the bound.
Values may be sent and summed in bfloat16 or wider, within the bound.
A program may use at most 64 MiB of HBM per device.

v0:
```python
import jax
import jax.numpy as jnp
from jax import lax
from jax.sharding import PartitionSpec as P

HEADS = 24
KV_HEADS = 8
HEAD_DIM = 64
TOP = 2
EPS = 1e-05


def passed_along(value, axis, steps):
    count = lax.axis_size(axis)
    initial, last = (max(0, -steps), min(count, count - steps))
    return lax.ppermute(value, axis, [(source, source + steps) for source in range(initial, last)])


def rms_scale(inputs, scale_row):
    inputs = inputs.astype(jnp.float32)
    inverse = lax.rsqrt(jnp.mean(inputs * inputs, axis=-1, keepdims=True) + EPS)
    return inputs * inverse * scale_row


def segment_of(req_lengths, positions):
    request_ends = jnp.cumsum(req_lengths, dtype=jnp.int32)
    return jnp.sum((request_ends[None, :] <= positions[:, None]).astype(jnp.int32), axis=1)


def product(left, right):
    return jnp.dot(left, right, preferred_element_type=jnp.float32)


def attend(soft_state, queries, key_block, allowed):
    maxima, totals, numerators = soft_state
    kv_width = key_block.shape[1] // 2
    key_rows = key_block[:, :kv_width].reshape(
        key_block.shape[0], queries.shape[1], queries.shape[3]
    )
    value_rows = key_block[:, kv_width:].reshape(
        key_block.shape[0], queries.shape[1], queries.shape[3]
    )
    scores = jnp.einsum(
        "tkgd,skd->tkgs", queries, key_rows, preferred_element_type=jnp.float32
    ) * queries.shape[3] ** (-0.5)
    if allowed is not None:
        scores = jnp.where(allowed[:, None, None, :], scores, -jnp.inf)
    new_max = jnp.maximum(maxima, jnp.max(scores, axis=-1))
    rescale = jnp.exp(maxima - new_max)
    weights = jnp.exp(scores - new_max[..., None])
    totals = totals * rescale + jnp.sum(weights, axis=-1)
    numerators = numerators * rescale[..., None] + jnp.einsum(
        "tkgs,skd->tkgd",
        weights.astype(jnp.bfloat16),
        value_rows,
        preferred_element_type=jnp.float32,
    )
    return (new_max, totals, numerators)


def on_device(
    layer_input,
    attn_gain,
    w_query,
    w_keyval,
    w_output,
    prefix_cache,
    lengths,
    moe_gain,
    w_router,
    routes,
    w_expert_in,
    w_expert_out,
):
    tokens = layer_input[0]
    row_count = tokens.shape[0]
    model_width = tokens.shape[1]
    group_share = HEADS // KV_HEADS
    normed = rms_scale(tokens, attn_gain).astype(jnp.bfloat16)
    columns = normed
    query_full = product(columns, lax.all_gather(w_query, "tok", axis=0, tiled=True))
    keyval_full = product(columns, lax.all_gather(w_keyval, "tok", axis=0, tiled=True))
    queries = query_full.astype(jnp.bfloat16).reshape(row_count, KV_HEADS, group_share, HEAD_DIM)
    keyval = keyval_full.astype(jnp.bfloat16)
    position = lax.axis_index("tok")
    positions = position * row_count + jnp.arange(row_count, dtype=jnp.int32)
    req_lengths = lengths[0]
    own_seg = segment_of(req_lengths, positions)
    before_seg = jnp.where(
        positions >= row_count, segment_of(req_lengths, positions - row_count), -1
    )
    earlier = passed_along(keyval, "tok", 1)
    near_block = jnp.concatenate([earlier, keyval], axis=0)
    near_seg = jnp.concatenate([before_seg, own_seg])
    near_pos = jnp.concatenate([positions - row_count, positions])
    allowed = (near_seg[None, :] == own_seg[:, None]) & (near_pos[None, :] <= positions[:, None])
    soft_state = (
        jnp.full((row_count, KV_HEADS, group_share), -jnp.inf, jnp.float32),
        jnp.zeros((row_count, KV_HEADS, group_share), jnp.float32),
        jnp.zeros((row_count, KV_HEADS, group_share, HEAD_DIM), jnp.float32),
    )
    soft_state = attend(soft_state, queries, near_block, allowed)
    prefix_whole = lax.all_gather(prefix_cache[0], "tok", axis=0, tiled=True)
    maxima, totals, numerators = attend(soft_state, queries, prefix_whole, None)
    attended = (
        (numerators / totals[..., None]).astype(jnp.bfloat16).reshape(row_count, HEADS * HEAD_DIM)
    )
    columns = attended
    residual = tokens.astype(jnp.float32) + product(
        columns, lax.all_gather(w_output, "tok", axis=0, tiled=True)
    )
    normed2 = rms_scale(residual, moe_gain).astype(jnp.bfloat16)
    logits = product(normed2, w_router)
    experts = w_router.shape[1]
    chosen = routes[0]
    expert_marks = chosen[:, :, None] == jnp.arange(experts, dtype=jnp.int32)
    picked = jnp.sum(jnp.where(expert_marks, logits[:, None, :], 0.0), axis=-1)
    scores = jax.nn.sigmoid(picked)
    gate_weights = scores / jnp.sum(scores, axis=-1, keepdims=True)
    capacity = max(4, 5 * row_count * TOP // (4 * experts))
    flat_routes = chosen.reshape(-1)
    flat_marks = expert_marks.reshape(-1, experts).astype(jnp.int32)
    prior_count = jnp.cumsum(flat_marks, axis=0, dtype=jnp.int32) - flat_marks
    slot_index = jnp.sum(prior_count * flat_marks, axis=1)
    target = flat_routes * capacity + slot_index
    copies = flat_routes.shape[0]
    slot_match = target[None, :] == jnp.arange(experts * capacity, dtype=jnp.int32)[:, None]
    filled = jnp.any(slot_match, axis=1)
    source = jnp.sum(jnp.where(slot_match, jnp.arange(copies, dtype=jnp.int32)[None, :], 0), axis=1)
    outgoing = jnp.where(filled[:, None], normed2[source // TOP], 0).reshape(
        experts, capacity, model_width
    )
    to_send = jnp.repeat(outgoing, 2, axis=0)
    arrived = lax.all_to_all(to_send, "tok", split_axis=0, concat_axis=0, tiled=True)
    flat_rows = arrived.reshape(-1, model_width)
    columns = flat_rows
    gate_up = product(columns, lax.all_gather(w_expert_in[0], "grp", axis=0, tiled=True))
    half_units = gate_up.shape[1] // 2
    act = (jax.nn.silu(gate_up[:, :half_units]) * gate_up[:, half_units:]).astype(jnp.bfloat16)
    columns = act
    partial_out = product(columns, lax.all_gather(w_expert_out[0], "grp", axis=0, tiled=True))
    returned = lax.all_to_all(
        partial_out.reshape(arrived.shape).astype(jnp.bfloat16),
        "tok",
        split_axis=0,
        concat_axis=0,
        tiled=True,
    ).astype(jnp.float32)
    results = jnp.sum(returned.reshape(experts, 2, capacity, model_width), axis=1).astype(
        jnp.bfloat16
    )
    gathered = results.reshape(experts * capacity, model_width)[target].astype(jnp.float32)
    weighted = jnp.sum(
        gathered.reshape(row_count, TOP, model_width) * gate_weights[:, :, None], axis=1
    )
    hidden = (residual + weighted).astype(jnp.bfloat16)
    return (hidden[None], keyval[None])


def solution(mesh):
    in_specs = (
        P("grp", "tok", None),
        P(),
        P("tok", None),
        P("tok", None),
        P("tok", None),
        P("grp", "tok", None),
        P("grp", None),
        P(),
        P(),
        P("grp", "tok", None),
        P("tok", "grp", None),
        P("tok", "grp", None),
    )
    out_specs = (P("grp", "tok", None), P("grp", "tok", None))
    return jax.shard_map(
        on_device, mesh=mesh, in_specs=in_specs, out_specs=out_specs, check_vma=False
    )
```

profile of v0, /device:TPU:1, one launch (start us, length us, event | category | flops | bytes accessed | tf_op | source)
XLA Modules:
  0.0 535.8 jit_solution(8123321330734562649)
XLA Ops:
  15.7 63.8 %all-gather.10.cloned.1.call-done = bf16[1536,1024]{1,0:T(8,128)(2,1)} async-done(((bf16[48,1024]{1,0:T(8,128)(2,1)}), bf16[1536,1024]{1,0:T(8,128)(2,1)}) %all-gather.10.cloned.1.call-update) | async-done | bytes 3145744 | tf_op jit(solution)/shard_map/all_gather | solution.py:82
  79.5 2.9 convolution_convert_fusion.2
  82.4 2.7 collective-permute-start
  85.4 59.2 %all-gather.16.cloned.1.call-done = bf16[1,512,1024]{2,1,0:T(8,128)(2,1)} async-done(((bf16[1,16,1024]{2,1,0:T(8,128)(2,1)}), bf16[1,512,1024]{2,1,0:T(8,128)(2,1)}) %all-gather.16.cloned.1.call-update) | async-done | bytes 1048592 | tf_op jit(solution)/shard_map/all_gather | solution.py:103
  147.6 65.7 %all-gather.12.cloned.1.call-done = bf16[1536,1536]{1,0:T(8,128)(2,1)} async-done(((bf16[48,1536]{1,0:T(8,128)(2,1)}), bf16[1536,1536]{1,0:T(8,128)(2,1)}) %all-gather.12.cloned.1.call-update) | async-done | bytes 4718608 | tf_op jit(solution)/shard_map/all_gather | solution.py:81
  213.3 3.5 convolution_convert_fusion.1
  222.7 3.2 fusion.6
  228.3 2.5 fusion.18
  230.8 51.3 %all-gather.14.cloned.1.call-done = bf16[1536,1536]{1,0:T(8,128)(2,1)} async-done(((bf16[48,1536]{1,0:T(8,128)(2,1)}), bf16[1536,1536]{1,0:T(8,128)(2,1)}) %all-gather.14.cloned.1.call-update) | async-done | bytes 4718608 | tf_op jit(solution)/shard_map/all_gather | solution.py:110
  282.1 3.6 multiply_reduce_fusion.1
  286.9 2.9 gather_fusion
  293.7 6.4 %all-to-all-start = ((bf16[32,30,1536]{2,1,0:T(8,128)(2,1)}), bf16[32,30,1536]{2,1,0:T(8,128)(2,1)}, u32[]{:S(2)}, u32[]{:S(2)}) async-start(bf16[32,30,1536]{2,1,0:T(8,128)(2,1)} %bitcast.112), calls=%async_computation | async-start | bytes 6291456 | tf_op jit(solution)/shard_map/all_to_all | solution.py:134
  300.7 71.3 %all-to-all-done = bf16[32,30,1536]{2,1,0:T(8,128)(2,1)} async-done(((bf16[32,30,1536]{2,1,0:T(8,128)(2,1)}), bf16[32,30,1536]{2,1,0:T(8,128)(2,1)}, u32[]{:S(2)}, u32[]{:S(2)}) %all-to-all-start) | async-done | bytes 2949152 | tf_op jit(solution)/shard_map/all_to_all | solution.py:134
  372.0 4.4 reshape.322
  376.4 7.9 %fusion.13 = f32[960,1024]{1,0:T(8,128)} fusion(bf16[960,1536]{1,0:T(8,128)(2,1)} %reshape.322, bf16[1,1536,1024]{2,1,0:T(8,128)(2,1)} %all-gather.18.cloned.1.call-done), kind=kOutput, calls=%fused_computation.19 | convolution fusion | flops 3019898880 | bytes 10027008 | tf_op jit(solution)/shard_map/dot_general | solution.py:31
  384.3 40.2 %all-gather.20.cloned.1.call-done = bf16[1,512,1536]{2,1,0:T(8,128)(2,1)} async-done(((bf16[1,64,1536]{2,1,0:T(8,128)(2,1)}), bf16[1,512,1536]{2,1,0:T(8,128)(2,1)}) %all-gather.20.cloned.1.call-update) | async-done | bytes 1572880 | tf_op jit(solution)/shard_map/all_gather | solution.py:141
  424.5 5.9 %convolution_convert_fusion = bf16[960,1536]{1,0:T(8,128)(2,1)} fusion(bf16[1,512,1536]{2,1,0:T(8,128)(2,1)} %all-gather.20.cloned.1.call-done, f32[960,1024]{1,0:T(8,128)} %fusion.13), kind=kOutput, calls=%fused_computation.15 | convolution fusion | flops 1514373120 | bytes 8454144 | tf_op jit(solution)/shard_map/dot_general | solution.py:31
  430.5 4.5 convert_element_type.85
  434.9 9.0 %all-to-all-start.1 = ((bf16[32,30,1536]{2,1,0:T(8,128)(2,1)}), bf16[32,30,1536]{2,1,0:T(8,128)(2,1)}, u32[]{:S(2)}, u32[]{:S(2)}) async-start(bf16[32,30,1536]{2,1,0:T(8,128)(2,1)} %convert_element_type.85), calls=%async_computation.1 | async-start | bytes 6291456 | tf_op jit(solution)/shard_map/all_to_all | solution.py:142
  444.7 71.1 %all-to-all-done.1 = bf16[32,30,1536]{2,1,0:T(8,128)(2,1)} async-done(((bf16[32,30,1536]{2,1,0:T(8,128)(2,1)}), bf16[32,30,1536]{2,1,0:T(8,128)(2,1)}, u32[]{:S(2)}, u32[]{:S(2)}) %all-to-all-start.1) | async-done | bytes 2949152 | tf_op jit(solution)/shard_map/all_to_all | solution.py:142
  515.8 2.5 bitcast_reduce_fusion.1
  518.7 2.8 gather_fusion.1
  521.5 2.8 reshape.326
  524.4 3.6 multiply_reduce_fusion
  (87 shorter events, 27.5 us)
Async XLA Ops:
  7.2 437.1 %copy-start = (bf16[1536,16]{0,1:T(8,128)(2,1)S(1)}, bf16[1536,16]{0,1:T(8,128)(2,1)}, u32[]{:S(2)}) copy-start(bf16[1536,16]{0,1:T(8,128)(2,1)} %param.20) | copy-start | bytes 147460
  7.2 72.3 %all-gather.10.cloned.1.call-start = ((), (), s32[]{:S(2)}) async-start(), calls=%async_computation.2 | async-start | bytes 3244032 | tf_op jit(solution)/shard_map/all_gather | solution.py:82
  7.9 136.7 %all-gather.16.cloned.1.call-start = ((), (), s32[]{:S(2)}) async-start(), calls=%async_computation.5 | async-start | bytes 1081344 | tf_op jit(solution)/shard_map/all_gather | solution.py:103
  8.7 204.6 %all-gather.12.cloned.1.call-start = ((), (), s32[]{:S(2)}) async-start(), calls=%async_computation.3 | async-start | bytes 4866048 | tf_op jit(solution)/shard_map/all_gather | solution.py:81
  9.4 272.7 %all-gather.14.cloned.1.call-start = ((), (), s32[]{:S(2)}) async-start(), calls=%async_computation.4 | async-start | bytes 4866048 | tf_op jit(solution)/shard_map/all_gather | solution.py:110
  10.0 366.5 %all-gather.18.cloned.1.call-start = ((), (), s32[]{:S(2)}) async-start(), calls=%async_computation.6 | async-start | bytes 3538944 | tf_op jit(solution)/shard_map/all_gather | solution.py:137
  82.4 64.1 %copy-start.5 = (bf16[192,1024]{1,0:T(8,128)(2,1)}, bf16[192,1024]{1,0:T(8,128)(2,1)S(1)}, u32[]{:S(2)}) copy-start(bf16[192,1024]{1,0:T(8,128)(2,1)S(1)} %convolution_convert_fusion.2) | copy-start | bytes 1179652
  82.4 64.0 %collective-permute-start = (bf16[192,1024]{1,0:T(8,128)(2,1)S(1)}, bf16[192,1024]{1,0:T(8,128)(2,1)S(1)}, u32[]{:S(2)}, u32[]{:S(2)}) collective-permute-start(bf16[192,1024]{1,0:T(8,128)(2,1)S(1)} %convolution_convert_fusion.2), channel_id=1, source_target_pairs={{0,1},{1,2},{2,3},{3,4},{4,5},{5,6},{6,7},{7,8},{8,9},{9,10},{10,1... | collective-permute-start | bytes 1179656 | tf_op jit(solution)/shard_map/ppermute | solution.py:16
  145.9 67.4 %copy-start.3 = (bf16[1,192,1536]{2,1,0:T(8,128)(2,1)S(1)}, bf16[1,192,1536]{2,1,0:T(8,128)(2,1)}, u32[]{:S(2)}) copy-start(bf16[1,192,1536]{2,1,0:T(8,128)(2,1)} %param.12) | copy-start | bytes 1769476
  145.9 67.4 %copy-start.8 = (f32[1536]{0:T(1024)S(1)}, f32[1536]{0:T(1024)}, u32[]{:S(2)}) copy-start(f32[1536]{0:T(1024)} %param.13) | copy-start | bytes 18436
  226.0 2.3 copy-start.4
  282.1 4.7 copy-start.7
  285.7 1.1 copy-start.1
  293.7 78.3 %all-to-all-start = ((bf16[32,30,1536]{2,1,0:T(8,128)(2,1)}), bf16[32,30,1536]{2,1,0:T(8,128)(2,1)}, u32[]{:S(2)}, u32[]{:S(2)}) async-start(bf16[32,30,1536]{2,1,0:T(8,128)(2,1)} %bitcast.112), calls=%async_computation | async-start | bytes 6291456 | tf_op jit(solution)/shard_map/all_to_all | solution.py:134
  300.1 124.4 %all-gather.20.cloned.1.call-start = ((), (), s32[]{:S(2)}) async-start(), calls=%async_computation.7 | async-start | bytes 1769472 | tf_op jit(solution)/shard_map/all_gather | solution.py:141
  434.9 9.0 %copy-start.6 = (s32[1,192,2]{1,2,0:T(2,128)S(1)}, s32[1,192,2]{1,2,0:T(2,128)}, u32[]{:S(2)}) copy-start(s32[1,192,2]{1,2,0:T(2,128)} %param.21) | copy-start | bytes 4612
  434.9 80.9 %all-to-all-start.1 = ((bf16[32,30,1536]{2,1,0:T(8,128)(2,1)}), bf16[32,30,1536]{2,1,0:T(8,128)(2,1)}, u32[]{:S(2)}, u32[]{:S(2)}) async-start(bf16[32,30,1536]{2,1,0:T(8,128)(2,1)} %convert_element_type.85), calls=%async_computation.1 | async-start | bytes 6291456 | tf_op jit(solution)/shard_map/all_to_all | solution.py:142
  524.4 3.6 copy-start.2
Sparse Core Ops, SparseCore 0:
  9.8 69.5 all-gather.9
  81.3 63.2 all-gather.15
  146.5 66.7 all-gather.11
  215.0 67.0 all-gather.13
  284.5 88.3 all-gather.17
  375.4 49.0 all-gather.19
where the time goes:
time: 536 us
  waiting for transfers between devices  426 us (79%)
  matrix products  33 us (6%)
  local copies, waits for them, and re-layouts  28.2 us (5%)
  starting transfers between devices  18.5 us (3%)
  other arithmetic  15.3 us (3%)
  between operations  14.5 us (3%)
    all_to_all x1, waiting for transfers between devices, on_device(): lax.all_to_all(to_send, 'tok', split_axis=0, concat_axis=0, tiled=True)  71.3 us
    all_to_all x1, waiting for transfers between devices, on_device(): lax.all_to_all(partial_out.reshape(arrived.shape).astype(jnp.bfloat16), '...  71.1 us
    all_gather x1, waiting for transfers between devices, on_device(): lax.all_gather(w_query, 'tok', axis=0, tiled=True)  65.7 us
    all_gather x1, waiting for transfers between devices, on_device(): lax.all_gather(w_keyval, 'tok', axis=0, tiled=True)  63.8 us
    all_gather x1, waiting for transfers between devices, on_device(): prefix_whole = lax.all_gather(prefix_cache[0], 'tok', axis=0, tiled=True)  59.2 us
    all_gather x1, waiting for transfers between devices, on_device(): lax.all_gather(w_output, 'tok', axis=0, tiled=True)  51.3 us
    all_gather x1, waiting for transfers between devices, on_device(): lax.all_gather(w_expert_out[0], 'grp', axis=0, tiled=True)  40.2 us
    dot_general x6, matrix products, product(): return jnp.dot(left, right, preferred_element_type=jnp.float32)  24 us
  transfers between devices with their start and end apart: 9, of which 7 were waited for; matrix products, arithmetic and copies ran while one was open for 10% of the time, Pallas kernels for 0%

commit v1 on v0

--- a/solution.py
+++ b/solution.py
@@ -138,7 +138,16 @@
     half_units = gate_up.shape[1] // 2
     act = (jax.nn.silu(gate_up[:, :half_units]) * gate_up[:, half_units:]).astype(jnp.bfloat16)
     columns = act
-    partial_out = product(columns, lax.all_gather(w_expert_out[0], "grp", axis=0, tiled=True))
+
+    def obtain_figure(sheet, dev_axis, dim_at):
+        return jnp.concatenate(
+            lax.all_to_all(
+                jnp.stack([sheet for _ in range(lax.axis_size(dev_axis))], axis=0), dev_axis, 0, 0
+            ),
+            axis=dim_at,
+        )
+
+    partial_out = product(columns, obtain_figure(w_expert_out[0], "grp", 0))
     returned = lax.all_to_all(
         partial_out.reshape(arrived.shape).astype(jnp.bfloat16),
         "tok",

time: 536 us -> 515 us (0.961)
  waiting for transfers between devices: 426 us -> 396 us
  starting transfers between devices: 18.5 us -> 28.4 us
    all_gather x1 -> x0, waiting for transfers between devices: 40.2 us -> none  [on_device(): lax.all_gather(w_expert_out[0], 'grp', axis=0, tiled=True)]
    all_to_all x0 -> x1, waiting for transfers between devices: none -> 9.03 us  [obtain_figure(): lax.all_to_all(jnp.stack([sheet for _ in range(lax.axis_size(dev_axis))],...]
    all_to_all x0 -> x1, starting transfers between devices: none -> 6.15 us  [obtain_figure(): lax.all_to_all(jnp.stack([sheet for _ in range(lax.axis_size(dev_axis))],...]
  transfers between devices with their start and end apart: 9 -> 9, of which waited for: 7 -> 8; matrix products, arithmetic and copies ran while one was open for 10% -> 8% of each run, Pallas kernels for 0% -> 0%
where the time goes in v1:
time: 515 us; the launch traced here: 514 us
  waiting for transfers between devices  396 us (77%)
  local copies, waits for them, and re-layouts  29.6 us (6%)
  starting transfers between devices  28.4 us (6%)
  matrix products  28.2 us (5%)
  other arithmetic  16 us (3%)
  between operations  15.6 us (3%)
    all_to_all x1, waiting for transfers between devices, on_device(): lax.all_to_all(to_send, 'tok', split_axis=0, concat_axis=0, tiled=True)  71.3 us
    all_to_all x1, waiting for transfers between devices, on_device(): lax.all_to_all(partial_out.reshape(arrived.shape).astype(jnp.bfloat16), '...  71 us
    all_gather x1, waiting for transfers between devices, on_device(): lax.all_gather(w_query, 'tok', axis=0, tiled=True)  65.7 us
    all_gather x1, waiting for transfers between devices, on_device(): lax.all_gather(w_keyval, 'tok', axis=0, tiled=True)  64.4 us
    all_gather x1, waiting for transfers between devices, on_device(): prefix_whole = lax.all_gather(prefix_cache[0], 'tok', axis=0, tiled=True)  59.2 us
    all_gather x1, waiting for transfers between devices, on_device(): lax.all_gather(w_output, 'tok', axis=0, tiled=True)  51.1 us
    dot_general x6, matrix products, product(): return jnp.dot(left, right, preferred_element_type=jnp.float32)  19.2 us
    all_to_all x1, starting transfers between devices, on_device(): lax.all_to_all(partial_out.reshape(arrived.shape).astype(jnp.bfloat16), '...  12.7 us
  transfers between devices with their start and end apart: 9, of which 8 were waited for; matrix products, arithmetic and copies ran while one was open for 8% of the time, Pallas kernels for 0%

profile of v1, /device:TPU:1, one launch (start us, length us, event | category | flops | bytes accessed | tf_op | source)
XLA Modules:
  0.0 513.6 jit_solution(6288355232546390912)
XLA Ops:
  15.9 64.4 %all-gather.8.cloned.1.call-done = bf16[1536,1024]{1,0:T(8,128)(2,1)} async-done(((bf16[48,1024]{1,0:T(8,128)(2,1)}), bf16[1536,1024]{1,0:T(8,128)(2,1)}) %all-gather.8.cloned.1.call-update) | async-done | bytes 3145744 | tf_op jit(solution)/shard_map/all_gather | solution.py:82
  80.3 2.9 convolution_convert_fusion.2
  83.2 2.7 collective-permute-start
  86.3 59.2 %all-gather.14.cloned.1.call-done = bf16[1,512,1024]{2,1,0:T(8,128)(2,1)} async-done(((bf16[1,16,1024]{2,1,0:T(8,128)(2,1)}), bf16[1,512,1024]{2,1,0:T(8,128)(2,1)}) %all-gather.14.cloned.1.call-update) | async-done | bytes 1048592 | tf_op jit(solution)/shard_map/all_gather | solution.py:103
  148.4 65.7 %all-gather.10.cloned.1.call-done = bf16[1536,1536]{1,0:T(8,128)(2,1)} async-done(((bf16[48,1536]{1,0:T(8,128)(2,1)}), bf16[1536,1536]{1,0:T(8,128)(2,1)}) %all-gather.10.cloned.1.call-update) | async-done | bytes 4718608 | tf_op jit(solution)/shard_map/all_gather | solution.py:81
  214.1 3.5 convolution_convert_fusion.1
  225.9 3.2 fusion.6
  229.1 2.5 fusion.17
  231.7 51.1 %all-gather.12.cloned.1.call-done = bf16[1536,1536]{1,0:T(8,128)(2,1)} async-done(((bf16[48,1536]{1,0:T(8,128)(2,1)}), bf16[1536,1536]{1,0:T(8,128)(2,1)}) %all-gather.12.cloned.1.call-update) | async-done | bytes 4718608 | tf_op jit(solution)/shard_map/all_gather | solution.py:110
  282.8 3.6 multiply_reduce_fusion.1
  287.6 2.9 gather_fusion
  294.3 6.6 %all-to-all-start = ((bf16[32,30,1536]{2,1,0:T(8,128)(2,1)}), bf16[32,30,1536]{2,1,0:T(8,128)(2,1)}, u32[]{:S(2)}, u32[]{:S(2)}) async-start(bf16[32,30,1536]{2,1,0:T(8,128)(2,1)} %bitcast.114), calls=%async_computation | async-start | bytes 6291456 | tf_op jit(solution)/shard_map/all_to_all | solution.py:134
  301.5 71.3 %all-to-all-done = bf16[32,30,1536]{2,1,0:T(8,128)(2,1)} async-done(((bf16[32,30,1536]{2,1,0:T(8,128)(2,1)}), bf16[32,30,1536]{2,1,0:T(8,128)(2,1)}, u32[]{:S(2)}, u32[]{:S(2)}) %all-to-all-start) | async-done | bytes 2949152 | tf_op jit(solution)/shard_map/all_to_all | solution.py:134
  374.1 6.1 %all-to-all-start.1 = ((bf16[8,64,1536]{2,1,0:T(8,128)(2,1)}), bf16[8,64,1536]{2,1,0:T(8,128)(2,1)S(1)}, u32[]{:S(2)}, u32[]{:S(2)}) async-start(bf16[8,64,1536]{2,1,0:T(8,128)(2,1)} %stack.3), calls=%async_computation.1 | async-start | bytes 3145728 | tf_op jit(solution)/shard_map/all_to_all | solution.py:144
  380.2 4.5 reshape.326
  385.5 6.0 %fusion.13 = f32[960,1024]{1,0:T(8,128)S(1)} fusion(bf16[960,1536]{1,0:T(8,128)(2,1)} %reshape.326, bf16[1,1536,1024]{2,1,0:T(8,128)(2,1)} %all-gather.16.cloned.1.call-done), kind=kOutput, calls=%fused_computation.19 | convolution fusion | flops 3019898880 | bytes 10027008 | tf_op jit(solution)/shard_map/dot_general | solution.py:31
  393.4 9.0 %all-to-all-done.1 = bf16[8,64,1536]{2,1,0:T(8,128)(2,1)S(1)} async-done(((bf16[8,64,1536]{2,1,0:T(8,128)(2,1)}), bf16[8,64,1536]{2,1,0:T(8,128)(2,1)S(1)}, u32[]{:S(2)}, u32[]{:S(2)}) %all-to-all-start.1) | async-done | bytes 1572896 | tf_op jit(solution)/shard_map/all_to_all | solution.py:144
  402.4 3.1 convolution_convert_fusion
  405.5 3.3 copy.63
  408.8 12.7 %all-to-all-start.2 = ((bf16[32,30,1536]{2,1,0:T(8,128)(2,1)}), bf16[32,30,1536]{2,1,0:T(8,128)(2,1)}, u32[]{:S(2)}, u32[]{:S(2)}) async-start(bf16[32,30,1536]{2,1,0:T(8,128)(2,1)} %copy.63), calls=%async_computation.2 | async-start | bytes 6291456 | tf_op jit(solution)/shard_map/all_to_all | solution.py:151
  422.4 71.0 %all-to-all-done.2 = bf16[32,30,1536]{2,1,0:T(8,128)(2,1)} async-done(((bf16[32,30,1536]{2,1,0:T(8,128)(2,1)}), bf16[32,30,1536]{2,1,0:T(8,128)(2,1)}, u32[]{:S(2)}, u32[]{:S(2)}) %all-to-all-start.2) | async-done | bytes 2949152 | tf_op jit(solution)/shard_map/all_to_all | solution.py:151
  496.3 2.8 gather_fusion.1
  499.1 2.8 reshape.331
  502.0 3.6 multiply_reduce_fusion
  (91 shorter events, 33.2 us)
Async XLA Ops:
  8.0 413.9 %copy-start = (bf16[1536,16]{0,1:T(8,128)(2,1)S(1)}, bf16[1536,16]{0,1:T(8,128)(2,1)}, u32[]{:S(2)}) copy-start(bf16[1536,16]{0,1:T(8,128)(2,1)} %param.20) | copy-start | bytes 147460
  8.0 72.3 %all-gather.8.cloned.1.call-start = ((), (), s32[]{:S(2)}) async-start(), calls=%async_computation.3 | async-start | bytes 3244032 | tf_op jit(solution)/shard_map/all_gather | solution.py:82
  8.7 136.7 %all-gather.14.cloned.1.call-start = ((), (), s32[]{:S(2)}) async-start(), calls=%async_computation.6 | async-start | bytes 1081344 | tf_op jit(solution)/shard_map/all_gather | solution.py:103
  9.5 204.6 %all-gather.10.cloned.1.call-start = ((), (), s32[]{:S(2)}) async-start(), calls=%async_computation.4 | async-start | bytes 4866048 | tf_op jit(solution)/shard_map/all_gather | solution.py:81
  10.2 272.6 %all-gather.12.cloned.1.call-start = ((), (), s32[]{:S(2)}) async-start(), calls=%async_computation.5 | async-start | bytes 4866048 | tf_op jit(solution)/shard_map/all_gather | solution.py:110
  83.2 64.0 %copy-start.5 = (bf16[192,1024]{1,0:T(8,128)(2,1)}, bf16[192,1024]{1,0:T(8,128)(2,1)S(1)}, u32[]{:S(2)}) copy-start(bf16[192,1024]{1,0:T(8,128)(2,1)S(1)} %convolution_convert_fusion.2) | copy-start | bytes 1179652
  83.2 64.0 %collective-permute-start = (bf16[192,1024]{1,0:T(8,128)(2,1)S(1)}, bf16[192,1024]{1,0:T(8,128)(2,1)S(1)}, u32[]{:S(2)}, u32[]{:S(2)}) collective-permute-start(bf16[192,1024]{1,0:T(8,128)(2,1)S(1)} %convolution_convert_fusion.2), channel_id=1, source_target_pairs={{0,1},{1,2},{2,3},{3,4},{4,5},{5,6},{6,7},{7,8},{8,9},{9,10},{10,1... | collective-permute-start | bytes 1179656 | tf_op jit(solution)/shard_map/ppermute | solution.py:16
  147.0 67.2 %copy-start.3 = (bf16[1,192,1536]{2,1,0:T(8,128)(2,1)S(1)}, bf16[1,192,1536]{2,1,0:T(8,128)(2,1)}, u32[]{:S(2)}) copy-start(bf16[1,192,1536]{2,1,0:T(8,128)(2,1)} %param.12) | copy-start | bytes 1769476
  147.0 67.2 %copy-start.9 = (f32[1536]{0:T(1024)S(1)}, f32[1536]{0:T(1024)}, u32[]{:S(2)}) copy-start(f32[1536]{0:T(1024)} %param.13) | copy-start | bytes 18436
  225.9 3.2 copy-start.4
  282.8 4.6 copy-start.8
  286.4 1.0 copy-start.1
  294.3 78.5 %copy-start.6 = (bf16[1,64,1536]{2,1,0:T(8,128)(2,1)S(1)}, bf16[1,64,1536]{2,1,0:T(8,128)(2,1)}, u32[]{:S(2)}) copy-start(bf16[1,64,1536]{2,1,0:T(8,128)(2,1)} %param.23) | copy-start | bytes 589828
  294.3 78.5 %all-to-all-start = ((bf16[32,30,1536]{2,1,0:T(8,128)(2,1)}), bf16[32,30,1536]{2,1,0:T(8,128)(2,1)}, u32[]{:S(2)}, u32[]{:S(2)}) async-start(bf16[32,30,1536]{2,1,0:T(8,128)(2,1)} %bitcast.114), calls=%async_computation | async-start | bytes 6291456 | tf_op jit(solution)/shard_map/all_to_all | solution.py:134
  300.9 84.6 %all-gather.16.cloned.1.call-start = ((), (), s32[]{:S(2)}) async-start(), calls=%async_computation.7 | async-start | bytes 3538944 | tf_op jit(solution)/shard_map/all_gather | solution.py:137
  374.1 28.3 %all-to-all-start.1 = ((bf16[8,64,1536]{2,1,0:T(8,128)(2,1)}), bf16[8,64,1536]{2,1,0:T(8,128)(2,1)S(1)}, u32[]{:S(2)}, u32[]{:S(2)}) async-start(bf16[8,64,1536]{2,1,0:T(8,128)(2,1)} %stack.3), calls=%async_computation.1 | async-start | bytes 3145728 | tf_op jit(solution)/shard_map/all_to_all | solution.py:144
  408.8 12.7 %copy-start.7 = (s32[1,192,2]{1,2,0:T(2,128)S(1)}, s32[1,192,2]{1,2,0:T(2,128)}, u32[]{:S(2)}) copy-start(s32[1,192,2]{1,2,0:T(2,128)} %param.21) | copy-start | bytes 4612
  408.8 84.6 %all-to-all-start.2 = ((bf16[32,30,1536]{2,1,0:T(8,128)(2,1)}), bf16[32,30,1536]{2,1,0:T(8,128)(2,1)}, u32[]{:S(2)}, u32[]{:S(2)}) async-start(bf16[32,30,1536]{2,1,0:T(8,128)(2,1)} %copy.63), calls=%async_computation.2 | async-start | bytes 6291456 | tf_op jit(solution)/shard_map/all_to_all | solution.py:151
  502.0 3.6 copy-start.2
Sparse Core Ops, SparseCore 0:
  10.7 69.5 all-gather.7
  82.2 63.2 all-gather.13
  147.3 66.7 all-gather.9
  215.8 66.9 all-gather.11
Sparse Core Ops, SparseCore 1:
  304.0 81.5 all-gather.15
